TPU v7x, 32 devices: a whole 2x2x4 slice. The times are simulated.
32 devices in a mesh: gx: 8 (over y, x, core), gy: 4 (over z).
Axes of the slice: x: 2, y: 2, z: 4, core: 2. Of those that a mesh axis runs over, the one named last changes fastest.
Arguments:
- checkpoint: float32 [27, 32, 64, 128], P(None, 'gx', 'gy'), may hold values from 0.0001 to 0.5, as said below
- later_adjoint: float32 [27, 32, 64, 128], P(None, 'gx', 'gy'), may hold values from -6 to 6
- resistance: float32 [32, 64, 128], P('gx', 'gy'), may hold values from 0.05 to 0.8
- solid_mask: int32 [32, 64, 128], P('gx', 'gy'), may hold values from 0 to 1, as said below
Outputs:
- adjoint_start: float32 [27, 32, 64, 128], P(None, 'gx', 'gy')
- sensitivity: float32 [32, 64, 128], P('gx', 'gy')
Inputs may be any that keep to these rules, and one draw needn't show every extreme that they name: `checkpoint`: positive populations near equilibrium, with mean x velocity rising along x. `solid_mask`: solid grains are balls inside aligned 8 x 8 x 8 bricks; every brick keeps fluid at its corners.
All inputs are finite; a program needn't handle non-finite values.
Results may differ from a plain program's by a relative error of at most 0.0003.
Values sent between devices are 32-bit elements; how exact they have to be, the bound alone decides.
A program may use at most 64 MiB of HBM per device.

v0:
```python
import functools

import jax
import jax.numpy as jnp
import numpy as np
from jax import lax
from jax.experimental import pallas as pl
from jax.experimental.pallas import tpu as pltpu
from jax.sharding import PartitionSpec as P

MESH = pl.DeviceIdType.MESH
STEPS = 4
BETA = 1.0 / 1.04
KAPPA = 2.0 - 1.0 / BETA
BODY_FORCE = 0.0001
FLOOR = 2e-4
GAIN = 25.0
SPEEDS = [(a, b, c) for a in (-1, 0, 1) for b in (-1, 0, 1) for c in (-1, 0, 1)]
WTABLE = (8.0 / 27.0, 2.0 / 27.0, 1.0 / 54.0, 1.0 / 216.0)
CLASS = [a * a + b * b + c * c for a, b, c in SPEEDS]
PAIRS = list(range(14, 27))
PW = [WTABLE[CLASS[i]] for i in PAIRS]
W0 = WTABLE[0]
DIRS = [(1, 0), (-1, 0), (0, 1), (0, -1), (1, 1), (1, -1), (-1, 1), (-1, -1)]
TILE = 8


def moving(dx, dy, sign):
    return [
        i
        for i, (a, b, c) in enumerate(SPEEDS)
        if (dx == 0 or a == sign * dx) and (dy == 0 or b == sign * dy)
    ]


def quad(xx, yy, zz, xy, xz, yz):
    xpy, xpz, ypz = xx + yy, xx + zz, yy + zz
    tot = xpy + zz
    s1, s2 = tot + xy, tot - xy
    a, b = xz + yz, xz - yz
    return [
        zz, ypz - yz, yy, ypz + yz,
        s2 - b, xpy - xy, s2 + b,
        xpz - xz, xx, xpz + xz,
        s1 - a, xpy + xy, s1 + a,
    ]


def linear(x, y, z):
    xmy, xpy = x - y, x + y
    return [z, y - z, y, y + z, xmy - z, xmy, xmy + z, x - z, x, x + z, xpy - z, xpy, xpy + z]


def even_moments(e):
    e14, e15, e16, e17, e18, e19, e20, e21, e22, e23, e24, e25, e26 = e
    a, b, n, c = e18 + e20, e24 + e26, e21 + e23, e15 + e17
    m, p, cy = a + e19, b + e25, c + e16
    mp = m + p
    xx = mp + (n + e22)
    yy = cy + mp
    zz = (e14 + c) + (a + b) + n
    d18, d24, d21, d15 = e20 - e18, e26 - e24, e23 - e21, e17 - e15
    total = xx + cy + e14
    return total, xx, yy, zz, p - m, d18 + d24 + d21, d15 + d24 - d18


def odd_moments(o):
    o14, o15, o16, o17, o18, o19, o20, o21, o22, o23, o24, o25, o26 = o
    m, p = o18 + o19 + o20, o24 + o25 + o26
    x = m + p + (o21 + o22 + o23)
    y = (o15 + o16 + o17) + p - m
    z = o14 + (o17 - o15) + (o20 - o18) + (o26 - o24) + (o23 - o21)
    return x, y, z


def by_class(values):
    sums = {}
    for i, v in zip(PAIRS, values):
        sums[CLASS[i]] = v if CLASS[i] not in sums else sums[CLASS[i]] + v
    return sums


def split(f):
    even = [f[i] + f[26 - i] for i in PAIRS]
    odd = [f[i] - f[26 - i] for i in PAIRS]
    return even, odd, f[13]


def prepare(even, odd, f0, resist):
    total, xx, yy, zz, xy, xz, yz = even_moments(even)
    rho = total + f0
    j = odd_moments(odd)
    force = [rho * BODY_FORCE - resist * j[0], -resist * j[1], -resist * j[2]]
    inv = 1.0 / rho
    v = [j[a] + 0.5 * force[a] for a in range(3)]
    u = [v[a] * inv for a in range(3)]
    uv = [u[0] * v[0], u[1] * v[1], u[2] * v[2], u[0] * v[1], u[0] * v[2], u[1] * v[2]]
    third = rho * (1.0 / 3.0)
    pi = [xx - third, yy - third, zz - third, xy, xz, yz]
    stress = [pi[k] - uv[k] for k in range(6)]
    trace = stress[0] + stress[1] + stress[2]
    base = rho - 1.5 * (uv[0] + uv[1] + uv[2])
    q0 = trace * (-1.0 / 3.0)
    q = quad(
        stress[0] + q0, stress[1] + q0, stress[2] + q0, 2.0 * stress[3], 2.0 * stress[4], 2.0 * stress[5]
    )
    q = [val + (1 - CLASS[i]) * q0 if CLASS[i] != 1 else val for i, val in zip(PAIRS, q)]
    low = base - 1.5 * trace
    t2 = quad(*[4.5 * pi[k] for k in range(3)], *[9.0 * pi[k] for k in range(3, 6)])
    cv = linear(*v)
    he = [even[n] - (2.0 * PW[n]) * (low + t2[n]) for n in range(13)]
    ho = [odd[n] - (6.0 * PW[n]) * cv[n] for n in range(13)]
    h0 = f0 - W0 * low
    qq = by_class([val * val for val in q])
    ss = 40.5 * (WTABLE[1] * qq[1] + WTABLE[2] * qq[2] + WTABLE[3] * qq[3]) + (20.25 * W0) * (q0 * q0)
    sh = q0 * h0
    for n in range(13):
        sh = sh + q[n] * he[n]
    sh = 4.5 * sh
    hs = by_class([he[n] * he[n] + ho[n] * ho[n] for n in range(13)])
    hh = (
        (0.5 / WTABLE[1]) * hs[1] + (0.5 / WTABLE[2]) * hs[2] + (0.5 / WTABLE[3]) * hs[3]
        + (1.0 / W0) * (h0 * h0)
    )
    size = ss + hh
    inv_size = 1.0 / jnp.maximum(size, FLOOR)
    ratio = sh * inv_size
    gamma = 1.0 / BETA - KAPPA * ratio
    return dict(
        even=even, odd=odd, f0=f0, resist=resist, rho=rho, j=j, force=force, inv=inv, v=v, u=u, uv=uv,
        stress=stress, trace=trace, base=base, q=q, q0=q0, he=he, ho=ho, h0=h0, size=size,
        inv_size=inv_size, ratio=ratio, gamma=gamma,
    )


def relax(s):
    bg = BETA * s["gamma"]
    keep = 1.0 - bg
    kap = bg - 2.0 * BETA
    u, v, force = s["u"], s["v"], s["force"]
    uf = u[0] * force[0] + u[1] * force[1] + u[2] * force[2]
    const = bg * s["base"] - 1.5 * kap * s["trace"] - (3.0 * (1.0 - BETA)) * uf
    src = 9.0 * (1.0 - BETA)
    b45, k45, b9, k9 = 4.5 * bg, 4.5 * kap, 9.0 * bg, 9.0 * kap
    uv, st = s["uv"], s["stress"]
    t = [b45 * uv[a] + k45 * st[a] + src * (u[a] * force[a]) for a in range(3)]
    for n, (a, b) in enumerate(((0, 1), (0, 2), (1, 2))):
        t.append(b9 * uv[3 + n] + k9 * st[3 + n] + src * (u[a] * force[b] + u[b] * force[a]))
    tq = quad(*t)
    ck = linear(*[bg * v[a] + (1.0 - BETA) * force[a] for a in range(3)])
    even = [keep * s["even"][n] + (2.0 * PW[n]) * (const + tq[n]) for n in range(13)]
    odd = [keep * s["odd"][n] + (6.0 * PW[n]) * ck[n] for n in range(13)]
    return even, odd, keep * s["f0"] + W0 * const


def pull(s, me, mo, m0):
    bg = BETA * s["gamma"]
    keep = 1.0 - bg
    kap = bg - 2.0 * BETA
    u, v, force, uv, st = s["u"], s["v"], s["force"], s["uv"], s["stress"]
    q, q0, he, ho, h0 = s["q"], s["q0"], s["he"], s["ho"], s["h0"]
    off = ((0, 1), (0, 2), (1, 2))

    keep_bar = m0 * s["f0"]
    for n in range(13):
        keep_bar = keep_bar + (me[n] * s["even"][n] + mo[n] * s["odd"][n])
    mom = even_moments([(2.0 * PW[n]) * me[n] for n in range(13)])
    const_bar = mom[0] + W0 * m0
    tb = mom[1:]
    kb = odd_moments([(6.0 * PW[n]) * mo[n] for n in range(13)])
    bg_bar = (
        const_bar * s["base"]
        + 4.5 * (tb[0] * uv[0] + tb[1] * uv[1] + tb[2] * uv[2])
        + 9.0 * (tb[3] * uv[3] + tb[4] * uv[4] + tb[5] * uv[5])
        + (kb[0] * v[0] + kb[1] * v[1] + kb[2] * v[2])
    )
    kap_bar = (
        -1.5 * s["trace"] * const_bar
        + 4.5 * (tb[0] * st[0] + tb[1] * st[1] + tb[2] * st[2])
        + 9.0 * (tb[3] * st[3] + tb[4] * st[4] + tb[5] * st[5])
    )
    gamma_bar = BETA * (bg_bar + kap_bar - keep_bar)
    base_bar = bg * const_bar
    uf_bar = (-3.0 * (1.0 - BETA)) * const_bar

    scaled = KAPPA * gamma_bar * s["inv_size"]
    sh_bar = -4.5 * scaled
    size_bar = jnp.where(s["size"] > FLOOR, scaled * s["ratio"], 0.0)
    by_w = {k: size_bar * (1.0 / WTABLE[k]) for k in (1, 2, 3)}
    heb = [by_w[CLASS[i]] * he[n] + sh_bar * q[n] for n, i in enumerate(PAIRS)]
    hob = [by_w[CLASS[i]] * ho[n] for n, i in enumerate(PAIRS)]
    h0b = (size_bar * (2.0 / W0)) * h0 + sh_bar * q0
    by_q = {k: size_bar * (81.0 * WTABLE[k]) for k in (1, 2, 3)}
    qb = [sh_bar * he[n] + by_q[CLASS[i]] * q[n] for n, i in enumerate(PAIRS)]
    q0b = sh_bar * h0 + (size_bar * (40.5 * W0)) * q0

    hm = even_moments([(2.0 * PW[n]) * heb[n] for n in range(13)])
    low_bar = -(hm[0] + W0 * h0b)
    t2 = [-x for x in hm[1:]]
    hv = odd_moments([(6.0 * PW[n]) * hob[n] for n in range(13)])
    qm = even_moments(qb)
    q_all = (qm[0] + q0b) * (1.0 / 3.0)
    base_bar = base_bar + low_bar
    k45, k9 = 4.5 * kap, 9.0 * kap
    common = -1.5 * (kap * const_bar + low_bar) - q_all
    pb = [k45 * tb[a] + 4.5 * t2[a] + qm[1 + a] + common for a in range(3)]
    pb += [k9 * tb[a] + 9.0 * t2[a] + 2.0 * qm[1 + a] for a in range(3, 6)]

    that = [9.0 * tb[k] for k in range(6)]
    qhat = [bg * that[k] + 9.0 * t2[k] - (2.0 if k < 3 else 1.0) * pb[k] for k in range(6)]

    def apply(m, x):
        return [
            m[0] * x[0] + m[3] * x[1] + m[4] * x[2],
            m[3] * x[0] + m[1] * x[1] + m[5] * x[2],
            m[4] * x[0] + m[5] * x[1] + m[2] * x[2],
        ]

    qu = apply(qhat, u)
    tf = apply(that, force)
    tu = apply(that, u)
    rest = [((1.0 - BETA) * tf[a] + uf_bar * force[a]) * s["inv"] for a in range(3)]
    usq = u[0] * u[0] + u[1] * u[1] + u[2] * u[2]
    rho_bar = (
        base_bar * (1.0 + 1.5 * usq)
        - (pb[0] + pb[1] + pb[2]) * (1.0 / 3.0)
        - 0.5 * (u[0] * qu[0] + u[1] * qu[1] + u[2] * qu[2])
        - (u[0] * rest[0] + u[1] * rest[1] + u[2] * rest[2])
    )
    b3 = 3.0 * base_bar
    vb = [bg * kb[a] - hv[a] + qu[a] - b3 * u[a] + rest[a] for a in range(3)]
    fb = [(1.0 - BETA) * (kb[a] + tu[a]) + uf_bar * u[a] + 0.5 * vb[a] for a in range(3)]
    rho_bar = rho_bar + BODY_FORCE * fb[0]
    jb = [vb[a] - s["resist"] * fb[a] for a in range(3)]
    resist_bar = -(s["j"][0] * fb[0] + s["j"][1] * fb[1] + s["j"][2] * fb[2])
    pq = quad(*pb)
    jl = linear(*jb)
    eb = [keep * me[n] + heb[n] + rho_bar + pq[n] for n in range(13)]
    ob = [keep * mo[n] + hob[n] + jl[n] for n in range(13)]
    return eb, ob, keep * m0 + h0b + rho_bar, resist_bar


def kernel(
    nx, ny, cp_ref, la_ref, res_ref, mask_ref, out_ref, sens_ref,
    g, st, aux, fl, acc, ys, yr, cs, cr, ys0, yr0, cs0, cr0, sums, aux_sens,
    send, recv, send0, recv0, sum_send, sum_recv, la_sem,
):
    ext_x, ext_y, lanes = res_ref.shape
    tiles = ext_y // TILE
    chunks = ext_x * tiles
    top, end = TILE, TILE + ext_y
    px, py = lax.axis_index("gx"), lax.axis_index("gy")

    def device(dx, dy):
        return (lax.rem(px + (dx + nx), nx), lax.rem(py + (dy + ny), ny))

    partners = set((dx % nx, dy % ny) for dx, dy in DIRS)
    partners |= set((0, d) for d in range(1, ny)) | set((d, 0) for d in range(1, nx))
    partners = sorted(partners)
    barrier = pltpu.get_barrier_semaphore()
    for dx, dy in partners:
        pl.semaphore_signal(barrier, inc=1, device_id=device(dx, dy), device_id_type=MESH)

    la_copy = pltpu.make_async_copy(
        la_ref, g.at[2, :, pl.ds(1, ext_x), pl.ds(top, ext_y), :], la_sem
    )
    la_copy.start()
    fl[pl.ds(1, ext_x), pl.ds(top, ext_y), :] = 1.0 - mask_ref[...].astype(jnp.float32)

    def exchange(par, sign, first=False):
        ss, rs = (send0, recv0) if first else (send.at[par % 2], recv.at[par % 2])
        ysr, yrr = (ys0, yr0) if first else (ys.at[par % 2], yr.at[par % 2])
        csr, crr = (cs0, cr0) if first else (cs.at[par % 2], cr.at[par % 2])
        copies = []
        for d, (dx, dy) in enumerate(DIRS):
            if dy == 0:
                pops = moving(dx, 0, sign)
                lo = pops[0]
                near, far = (ext_x, 0) if dx > 0 else (1, ext_x + 1)
                rows = pl.ds(top, ext_y)
                src = g.at[par, pl.ds(lo, 9), near, rows, :]
                dst = g.at[par, pl.ds(lo, 9), far, rows, :]
            elif dx == 0:
                src, dst = ysr.at[d - 2], yrr.at[d - 2]
            else:
                src, dst = csr.at[d - 4], crr.at[d - 4]
            copies.append(
                pltpu.make_async_remote_copy(
                    src_ref=src, dst_ref=dst, send_sem=ss.at[d], recv_sem=rs.at[d],
                    device_id=device(dx, dy), device_id_type=MESH,
                )
            )
        if first:
            for d, (dx, dy) in enumerate(DIRS[:2]):
                near, far = (ext_x, 0) if dx > 0 else (1, ext_x + 1)
                rows = pl.ds(top, ext_y)
                copies.append(
                    pltpu.make_async_remote_copy(
                        src_ref=fl.at[near, rows, :], dst_ref=fl.at[far, rows, :],
                        send_sem=ss.at[8 + d], recv_sem=rs.at[8 + d],
                        device_id=device(dx, 0), device_id_type=MESH,
                    )
                )

        def pack_rows(unpack):
            for d, (dx, dy) in enumerate(DIRS):
                if dy == 0:
                    continue
                pops = moving(dx, dy, sign)
                if unpack:
                    row = top - 1 if dy > 0 else end
                    planes = [0 if dx > 0 else ext_x + 1] if dx else range(1, ext_x + 1)
                else:
                    row = end - 1 if dy > 0 else top
                    planes = [ext_x if dx > 0 else 1] if dx else range(1, ext_x + 1)
                box = (yrr if unpack else ysr) if dx == 0 else (crr if unpack else csr)
                k = d - 2 if dx == 0 else d - 4
                n = 0
                for i in pops:
                    for x in planes:
                        if unpack:
                            g[par, i, x, pl.ds(row, 1), :] = box[k, pl.ds(n, 1), :]
                        else:
                            box[k, pl.ds(n, 1), :] = g[par, i, x, pl.ds(row, 1), :]
                        n += 1
                if first:
                    for x in planes:
                        if unpack:
                            fl[x, pl.ds(row, 1), :] = box[k, pl.ds(n, 1), :]
                        else:
                            box[k, pl.ds(n, 1), :] = fl[x, pl.ds(row, 1), :]
                        n += 1

        def start():
            pack_rows(False)
            for copy in copies:
                copy.start()

        def finish():
            for copy in copies:
                copy.wait_recv()
            for copy in copies:
                copy.wait_send()
            pack_rows(True)

        return start, finish

    def place(c):
        x, t = c // tiles, lax.rem(c, tiles)
        return x, pl.multiple_of(t * TILE, TILE)

    def rolled(value, shift):
        return pltpu.roll(value, shift % lanes, 1) if shift else value

    def gather(par, x, row, sign):
        return [
            rolled(g[par, i, x + (1 - sign * a), pl.ds(row + (top - sign * b), TILE), :], sign * c)
            for i, (a, b, c) in enumerate(SPEEDS)
        ]

    def fluid_at(x, row, i):
        a, b, c = SPEEDS[i]
        return rolled(fl[x + (1 + a), pl.ds(row + (top + b), TILE), :], -c)

    def collided(f, x, row):
        solid = mask_ref[x, pl.ds(row, TILE), :] == 1
        even, odd, f0 = split(f)
        ne, no, n0 = relax(prepare(even, odd, f0, res_ref[x, pl.ds(row, TILE), :]))
        ne = [jnp.where(solid, even[n], ne[n]) * 0.5 for n in range(13)]
        no = [jnp.where(solid, -odd[n], no[n]) * 0.5 for n in range(13)]
        return ne, no, jnp.where(solid, f0, n0)

    def store_pairs(write, even, odd, f0):
        for n, i in enumerate(PAIRS):
            write(i, even[n] + odd[n])
            write(26 - i, even[n] - odd[n])
        write(13, f0)

    def into(par, x, row):
        def write(i, value):
            g[par, i, x + 1, pl.ds(row + top, TILE), :] = value
        return write

    def first_step(c, carry):
        x, row = place(c)
        f = [cp_ref[i, x, pl.ds(row, TILE), :] for i in range(27)]
        store_pairs(into(0, x, row), *collided(f, x, row))
        return carry

    lax.fori_loop(0, chunks, first_step, 0)
    start0, finish0 = exchange(0, 1)
    pl.semaphore_wait(barrier, len(partners))
    start0()
    la_copy.wait()
    start_la, finish_la = exchange(2, -1, first=True)
    start_la()
    finish0()
    for step in (1, 2):
        def forward_step(c, carry, step=step):
            x, row = place(c)
            f = gather((step - 1) % 2, x, row, 1)
            for i in range(27):
                st[step - 1, i, x, pl.ds(row, TILE), :] = f[i]
            store_pairs(into(step % 2, x, row), *collided(f, x, row))
            return carry

        lax.fori_loop(0, chunks, forward_step, 0)
        start, finish = exchange(step % 2, 1)
        start()
        if step == 1:
            finish_la()
        finish()

    def last_step(c, carry):
        x, row = place(c)
        f = gather(0, x, row, 1)
        for i in range(27):
            st[2, i, x, pl.ds(row, TILE), :] = f[i]
        ne, no, n0 = collided(f, x, row)
        for n, i in enumerate(PAIRS):
            if SPEEDS[i][0]:
                carry = carry + (
                    (ne[n] + no[n]) * fluid_at(x, row, i) - (ne[n] - no[n]) * fluid_at(x, row, 26 - i)
                )
        return carry

    part = lax.fori_loop(0, chunks, last_step, jnp.zeros((TILE, lanes), jnp.float32))

    def spread(slot, base, count, axis):
        copies = []
        for d in range(1, count):
            copies.append(
                pltpu.make_async_remote_copy(
                    src_ref=acc.at[slot], dst_ref=sums.at[base + d - 1],
                    send_sem=sum_send.at[base + d - 1], recv_sem=sum_recv.at[base + d - 1],
                    device_id=device(d, 0) if axis == 0 else device(0, d), device_id_type=MESH,
                )
            )
        return copies

    along_y, along_x = spread(0, 0, ny, 1), spread(1, ny - 1, nx, 0)
    acc[0] = part
    for copy in along_y:
        copy.start()

    def write_back(write, me, mo, m0, eb, ob, b0, solid):
        eb = [jnp.where(solid, me[n], eb[n]) for n in range(13)]
        ob = [jnp.where(solid, -mo[n], ob[n]) for n in range(13)]
        store_pairs(write, eb, ob, jnp.where(solid, m0, b0))

    def halves(m):
        even, odd, m0 = split(m)
        return [0.5 * e for e in even], [0.5 * o for o in odd], m0

    def adjoint_first(c, carry):
        x, row = place(c)
        rows = pl.ds(row, TILE)
        solid = mask_ref[x, rows, :] == 1
        f = [st[2, i, x, rows, :] for i in range(27)]
        s = prepare(*split(f), res_ref[x, rows, :])
        me, mo, m0 = halves(gather(2, x, row, -1))
        eb, ob, b0, rb = pull(s, me, mo, m0)
        write_back(into(1, x, row), me, mo, m0, eb, ob, b0, solid)
        sens_ref[x, rows, :] = jnp.where(solid, 0.0, rb)
        zero = jnp.zeros((TILE, lanes), jnp.float32)
        me, mo = [zero] * 13, [zero] * 13
        for n, i in enumerate(PAIRS):
            if SPEEDS[i][0]:
                ahead, behind = fluid_at(x, row, i), fluid_at(x, row, 26 - i)
                me[n], mo[n] = (0.5 * GAIN) * (ahead - behind), (0.5 * GAIN) * (ahead + behind)
        eb, ob, b0, rb = pull(s, me, mo, zero)

        def write(i, value):
            aux[i, x, rows, :] = value

        write_back(write, me, mo, zero, eb, ob, b0, solid)
        aux_sens[x, rows, :] = jnp.where(solid, 0.0, rb)
        return carry

    half = chunks // 2
    lax.fori_loop(0, half, adjoint_first, 0)
    for copy in along_y:
        copy.wait()
    total = acc[0]
    for d in range(ny - 1):
        total = total + sums[d]
    acc[1] = total
    for copy in along_x:
        copy.start()
    lax.fori_loop(half, chunks, adjoint_first, 0)
    for copy in along_x:
        copy.wait()
    for d in range(ny - 1, ny + nx - 2):
        total = total + sums[d]
    nodes = ext_x * ext_y * lanes * nx * ny
    mean = jnp.broadcast_to(jnp.sum(total, keepdims=True) * (1.0 / nodes), (TILE, lanes))

    def combine(c, carry):
        x, row = place(c)
        rows = pl.ds(row, TILE)
        inner = pl.ds(row + top, TILE)
        for i in range(27):
            g[1, i, x + 1, inner, :] = g[1, i, x + 1, inner, :] + mean * aux[i, x, rows, :]
        sens_ref[x, rows, :] = sens_ref[x, rows, :] + mean * aux_sens[x, rows, :]
        return carry

    lax.fori_loop(0, chunks, combine, 0)

    for step in (2, 1, 0):
        par = (step + 1) % 2
        start, finish = exchange(par, -1)
        start()
        finish()

        def adjoint_step(c, carry, step=step, par=par):
            x, row = place(c)
            rows = pl.ds(row, TILE)
            solid = mask_ref[x, rows, :] == 1
            if step:
                f = [st[step - 1, i, x, rows, :] for i in range(27)]
            else:
                f = [cp_ref[i, x, rows, :] for i in range(27)]
            s = prepare(*split(f), res_ref[x, rows, :])
            me, mo, m0 = halves(gather(par, x, row, -1))
            eb, ob, b0, rb = pull(s, me, mo, m0)

            def write(i, value):
                if step:
                    g[step % 2, i, x + 1, pl.ds(row + top, TILE), :] = value
                else:
                    out_ref[i, x, rows, :] = value

            write_back(write, me, mo, m0, eb, ob, b0, solid)
            sens_ref[x, rows, :] = sens_ref[x, rows, :] + jnp.where(solid, 0.0, rb)
            return carry

        lax.fori_loop(0, chunks, adjoint_step, 0)


def solution(mesh):
    nx, ny = mesh.shape["gx"], mesh.shape["gy"]

    def shards(checkpoint, later_adjoint, resistance, solid_mask):
        ext_x, ext_y, lanes = resistance.shape
        f32 = jnp.float32
        rows_x = 9 * ext_x
        vmem = pl.BlockSpec(memory_space=pltpu.VMEM)
        padded = (ext_x + 2, ext_y + 2 * TILE, lanes)
        count = nx + ny - 2
        return pl.pallas_call(
            functools.partial(kernel, nx, ny),
            out_shape=(
                jax.ShapeDtypeStruct(checkpoint.shape, f32),
                jax.ShapeDtypeStruct(resistance.shape, f32),
            ),
            in_specs=[vmem, pl.BlockSpec(memory_space=pl.ANY), vmem, vmem],
            out_specs=(vmem, vmem),
            scratch_shapes=[
                pltpu.VMEM((3, 27) + padded, f32),
                pltpu.VMEM((3, 27, ext_x, ext_y, lanes), f32),
                pltpu.VMEM((27, ext_x, ext_y, lanes), f32),
                pltpu.VMEM(padded, f32),
                pltpu.VMEM((2, TILE, lanes), f32),
                pltpu.VMEM((2, 2, rows_x, lanes), f32),
                pltpu.VMEM((2, 2, rows_x, lanes), f32),
                pltpu.VMEM((2, 4, 3, lanes), f32),
                pltpu.VMEM((2, 4, 3, lanes), f32),
                pltpu.VMEM((2, rows_x + ext_x, lanes), f32),
                pltpu.VMEM((2, rows_x + ext_x, lanes), f32),
                pltpu.VMEM((4, 4, lanes), f32),
                pltpu.VMEM((4, 4, lanes), f32),
                pltpu.VMEM((count, TILE, lanes), f32),
                pltpu.VMEM((ext_x, ext_y, lanes), f32),
                pltpu.SemaphoreType.DMA((2, 8)),
                pltpu.SemaphoreType.DMA((2, 8)),
                pltpu.SemaphoreType.DMA((10,)),
                pltpu.SemaphoreType.DMA((10,)),
                pltpu.SemaphoreType.DMA((count,)),
                pltpu.SemaphoreType.DMA((count,)),
                pltpu.SemaphoreType.DMA,
            ],
            compiler_params=pltpu.CompilerParams(
                collective_id=0, has_side_effects=True, vmem_limit_bytes=48 * 1024 * 1024
            ),
        )(checkpoint, later_adjoint, resistance, solid_mask)

    placed = (
        P(None, "gx", "gy", None),
        P(None, "gx", "gy", None),
        P("gx", "gy", None),
        P("gx", "gy", None),
    )
    return jax.shard_map(
        shards,
        mesh=mesh,
        in_specs=placed,
        out_specs=(P(None, "gx", "gy", None), P("gx", "gy", None)),
        check_vma=False,
    )
```

profile of v0, /device:TPU:0, one launch (start us, length us, event | category | flops | bytes accessed | tf_op | source)
XLA Modules:
  0.0 56.2 jit_solution(12170685474456344149)
XLA Ops:
  0.6 0.0 copy-start
  0.6 1.2 %copy-done = f32[27,4,16,128]{3,2,1,0:T(8,128)S(1)} copy-done((f32[27,4,16,128]{3,2,1,0:T(8,128)S(1)}, f32[27,4,16,128]{3,2,1,0:T(8,128)}, u32[]{:S(2)}) %copy-start) | copy-done | bytes 884760
  1.8 0.0 copy-start.1
  1.8 1.2 %copy-done.1 = f32[27,4,16,128]{3,2,1,0:T(8,128)S(1)} copy-done((f32[27,4,16,128]{3,2,1,0:T(8,128)S(1)}, f32[27,4,16,128]{3,2,1,0:T(8,128)}, u32[]{:S(2)}) %copy-start.1) | copy-done | bytes 884760
  3.0 0.0 copy-start.2
  3.0 0.8 %copy-done.2 = f32[4,16,128]{2,1,0:T(8,128)S(1)} copy-done((f32[4,16,128]{2,1,0:T(8,128)S(1)}, f32[4,16,128]{2,1,0:T(8,128)}, u32[]{:S(2)}) %copy-start.2) | copy-done | bytes 32792
  3.7 0.0 copy-start.3
  3.7 0.8 %copy-done.3 = s32[4,16,128]{2,1,0:T(8,128)S(1)} copy-done((s32[4,16,128]{2,1,0:T(8,128)S(1)}, s32[4,16,128]{2,1,0:T(8,128)}, u32[]{:S(2)}) %copy-start.3) | copy-done | bytes 32792
  4.5 50.1 %shard_map.59 = (f32[27,4,16,128]{3,2,1,0:T(8,128)S(1)}, f32[4,16,128]{2,1,0:T(8,128)S(1)}) custom-call(f32[27,4,16,128]{3,2,1,0:T(8,128)S(1)} %copy-done, f32[27,4,16,128]{3,2,1,0:T(8,128)S(1)} %copy-done.1, f32[4,16,128]{2,1,0:T(8,128)S(1)} %copy-done.2, s32[4,16,128]{2,1,0:T(8,128)S(1)} %copy-done.3), custom_call_target="tpu_custom_call" | custom-call | tf_op jit(solution)/shard_map/pallas_call | solution.py:550
  54.6 0.9 %copy.8 = f32[27,4,16,128]{3,2,1,0:T(8,128)} copy(f32[27,4,16,128]{3,2,1,0:T(8,128)S(1)} %get-tuple-element.4) | data formatting | bytes 1769472
  55.5 0.6 %copy.9 = f32[4,16,128]{2,1,0:T(8,128)} copy(f32[4,16,128]{2,1,0:T(8,128)S(1)} %get-tuple-element.5) | data formatting | bytes 65536
Async XLA Ops:
  0.6 1.2 %copy-start = (f32[27,4,16,128]{3,2,1,0:T(8,128)S(1)}, f32[27,4,16,128]{3,2,1,0:T(8,128)}, u32[]{:S(2)}) copy-start(f32[27,4,16,128]{3,2,1,0:T(8,128)} %cp_ref.1) | copy-start | bytes 2654212
  1.8 1.2 %copy-start.1 = (f32[27,4,16,128]{3,2,1,0:T(8,128)S(1)}, f32[27,4,16,128]{3,2,1,0:T(8,128)}, u32[]{:S(2)}) copy-start(f32[27,4,16,128]{3,2,1,0:T(8,128)} %la_ref.1) | copy-start | bytes 2654212
  3.0 0.8 %copy-start.2 = (f32[4,16,128]{2,1,0:T(8,128)S(1)}, f32[4,16,128]{2,1,0:T(8,128)}, u32[]{:S(2)}) copy-start(f32[4,16,128]{2,1,0:T(8,128)} %res_ref.1) | copy-start | bytes 98308
  3.7 0.8 %copy-start.3 = (s32[4,16,128]{2,1,0:T(8,128)S(1)}, s32[4,16,128]{2,1,0:T(8,128)}, u32[]{:S(2)}) copy-start(s32[4,16,128]{2,1,0:T(8,128)} %mask_ref.1) | copy-start | bytes 98308
where the time goes:
time: 56.5 us; the launch traced here: 56.2 us
  Pallas kernels  50.1 us (89%)
  local copies, waits for them, and re-layouts  5.37 us (10%)
  between operations  0.65 us (1%)
    pallas_call x1, Pallas kernels, shards(): pl.pallas_call(functools.partial(kernel, nx, ny), out_shape=(jax.ShapeDty...  50.1 us
    unnamed x10, local copies, waits for them, and re-layouts  5.37 us

commit v1 on v0

--- a/solution.py
+++ b/solution.py
@@ -241,9 +241,9 @@
 
 
 def kernel(
-    nx, ny, cp_ref, la_ref, res_ref, mask_ref, out_ref, sens_ref,
+    nx, ny, cp_hbm, la_ref, res_hbm, mask_hbm, out_ref, sens_ref, cp_ref, res_ref, mask_ref,
     g, st, aux, fl, acc, ys, yr, cs, cr, ys0, yr0, cs0, cr0, sums, aux_sens,
-    send, recv, send0, recv0, sum_send, sum_recv, la_sem,
+    send, recv, send0, recv0, sum_send, sum_recv, in_sem,
 ):
     ext_x, ext_y, lanes = res_ref.shape
     tiles = ext_y // TILE
@@ -262,9 +262,18 @@
         pl.semaphore_signal(barrier, inc=1, device_id=device(dx, dy), device_id_type=MESH)
 
     la_copy = pltpu.make_async_copy(
-        la_ref, g.at[2, :, pl.ds(1, ext_x), pl.ds(top, ext_y), :], la_sem
-    )
+        la_ref, g.at[2, :, pl.ds(1, ext_x), pl.ds(top, ext_y), :], in_sem.at[3]
+    )
+    loads = [
+        pltpu.make_async_copy(cp_hbm, cp_ref, in_sem.at[0]),
+        pltpu.make_async_copy(res_hbm, res_ref, in_sem.at[1]),
+        pltpu.make_async_copy(mask_hbm, mask_ref, in_sem.at[2]),
+    ]
+    for copy in loads:
+        copy.start()
     la_copy.start()
+    for copy in loads:
+        copy.wait()
     fl[pl.ds(1, ext_x), pl.ds(top, ext_y), :] = 1.0 - mask_ref[...].astype(jnp.float32)
 
     def exchange(par, sign, first=False):
@@ -302,10 +311,9 @@
                     )
                 )
 
-        def pack_rows(unpack):
-            for d, (dx, dy) in enumerate(DIRS):
-                if dy == 0:
-                    continue
+        def pack_rows(unpack, which):
+            for d in which:
+                dx, dy = DIRS[d]
                 pops = moving(dx, dy, sign)
                 if unpack:
                     row = top - 1 if dy > 0 else end
@@ -331,19 +339,59 @@
                             box[k, pl.ds(n, 1), :] = fl[x, pl.ds(row, 1), :]
                         n += 1
 
-        def start():
-            pack_rows(False)
-            for copy in copies:
+        def start_outer():
+            pack_rows(False, (4, 5, 6, 7))
+            for copy in copies[4:8] + copies[:2] + copies[8:]:
                 copy.start()
 
-        def finish():
-            for copy in copies:
+        def start_row(d):
+            pack_rows(False, (d,))
+            copies[d].start()
+
+        def finish(which):
+            done = copies[:2] + copies[4:] if which == 4 else [copies[which]]
+            for copy in done:
                 copy.wait_recv()
-            for copy in copies:
+            for copy in done:
                 copy.wait_send()
-            pack_rows(True)
-
-        return start, finish
+            pack_rows(True, (4, 5, 6, 7) if which == 4 else (which,))
+
+        return start_outer, start_row, finish
+
+    def sweep(body, flip, sends=None, waits=None):
+        early, late = (2, 3) if flip else (3, 2)
+        wide = ext_x - 2
+
+        def step(c, carry):
+            if waits is not None:
+                @pl.when(c == 2 * (tiles - 1))
+                def _():
+                    waits(early)
+            side = c < 2 * tiles
+            k = c - 2 * tiles
+            t = jnp.where(side, c // 2, k // wide)
+            x = jnp.where(side, lax.rem(c, 2) * (ext_x - 1), 1 + lax.rem(k + 2 * wide * tiles, wide))
+            if flip:
+                t = tiles - 1 - t
+            body(x, pl.multiple_of(t * TILE, TILE))
+            if sends is not None:
+                start_outer, start_row = sends
+
+                @pl.when(c == 2 * tiles - 1)
+                def _():
+                    start_outer()
+
+                @pl.when(c == 2 * tiles + wide - 1)
+                def _():
+                    start_row(early)
+            return carry
+
+        if waits is not None:
+            waits(4)
+            waits(late)
+        lax.fori_loop(0, chunks, step, 0)
+        if sends is not None:
+            sends[1](late)
 
     def place(c):
         x, t = c // tiles, lax.rem(c, tiles)
@@ -381,50 +429,49 @@
             g[par, i, x + 1, pl.ds(row + top, TILE), :] = value
         return write
 
-    def first_step(c, carry):
-        x, row = place(c)
+    def first_step(x, row):
         f = [cp_ref[i, x, pl.ds(row, TILE), :] for i in range(27)]
         store_pairs(into(0, x, row), *collided(f, x, row))
-        return carry
-
-    lax.fori_loop(0, chunks, first_step, 0)
-    start0, finish0 = exchange(0, 1)
+
+    start_outer, start_row, finish = exchange(0, 1)
+    sweep(first_step, 0)
     pl.semaphore_wait(barrier, len(partners))
-    start0()
+    start_outer()
+    start_row(3)
+    start_row(2)
     la_copy.wait()
-    start_la, finish_la = exchange(2, -1, first=True)
-    start_la()
-    finish0()
+    outer_la, row_la, finish_la = exchange(2, -1, first=True)
+    outer_la()
+    row_la(3)
+    row_la(2)
     for step in (1, 2):
-        def forward_step(c, carry, step=step):
-            x, row = place(c)
+        def forward_step(x, row, step=step):
             f = gather((step - 1) % 2, x, row, 1)
             for i in range(27):
                 st[step - 1, i, x, pl.ds(row, TILE), :] = f[i]
             store_pairs(into(step % 2, x, row), *collided(f, x, row))
-            return carry
-
-        lax.fori_loop(0, chunks, forward_step, 0)
-        start, finish = exchange(step % 2, 1)
-        start()
-        if step == 1:
-            finish_la()
-        finish()
-
-    def last_step(c, carry):
-        x, row = place(c)
+
+        start_outer, start_row, later = exchange(step % 2, 1)
+        sweep(forward_step, step % 2, (start_outer, start_row), finish)
+        finish = later
+    for d in (4, 3, 2):
+        finish_la(d)
+    acc[0] = jnp.zeros((TILE, lanes), jnp.float32)
+
+    def last_step(x, row):
         f = gather(0, x, row, 1)
         for i in range(27):
             st[2, i, x, pl.ds(row, TILE), :] = f[i]
         ne, no, n0 = collided(f, x, row)
+        flux = acc[0]
         for n, i in enumerate(PAIRS):
             if SPEEDS[i][0]:
-                carry = carry + (
+                flux = flux + (
                     (ne[n] + no[n]) * fluid_at(x, row, i) - (ne[n] - no[n]) * fluid_at(x, row, 26 - i)
                 )
-        return carry
-
-    part = lax.fori_loop(0, chunks, last_step, jnp.zeros((TILE, lanes), jnp.float32))
+        acc[0] = flux
+
+    sweep(last_step, 1, None, finish)
 
     def spread(slot, base, count, axis):
         copies = []
@@ -439,7 +486,6 @@
         return copies
 
     along_y, along_x = spread(0, 0, ny, 1), spread(1, ny - 1, nx, 0)
-    acc[0] = part
     for copy in along_y:
         copy.start()
 
@@ -495,25 +541,20 @@
     nodes = ext_x * ext_y * lanes * nx * ny
     mean = jnp.broadcast_to(jnp.sum(total, keepdims=True) * (1.0 / nodes), (TILE, lanes))
 
-    def combine(c, carry):
-        x, row = place(c)
+    def combine(x, row):
         rows = pl.ds(row, TILE)
-        inner = pl.ds(row + top, TILE)
+        at = pl.ds(row + top, TILE)
         for i in range(27):
-            g[1, i, x + 1, inner, :] = g[1, i, x + 1, inner, :] + mean * aux[i, x, rows, :]
+            g[1, i, x + 1, at, :] = g[1, i, x + 1, at, :] + mean * aux[i, x, rows, :]
         sens_ref[x, rows, :] = sens_ref[x, rows, :] + mean * aux_sens[x, rows, :]
-        return carry
-
-    lax.fori_loop(0, chunks, combine, 0)
+
+    start_outer, start_row, finish = exchange(1, -1)
+    sweep(combine, 0, (start_outer, start_row))
 
     for step in (2, 1, 0):
         par = (step + 1) % 2
-        start, finish = exchange(par, -1)
-        start()
-        finish()
-
-        def adjoint_step(c, carry, step=step, par=par):
-            x, row = place(c)
+
+        def adjoint_step(x, row, step=step, par=par):
             rows = pl.ds(row, TILE)
             solid = mask_ref[x, rows, :] == 1
             if step:
@@ -532,9 +573,13 @@
 
             write_back(write, me, mo, m0, eb, ob, b0, solid)
             sens_ref[x, rows, :] = sens_ref[x, rows, :] + jnp.where(solid, 0.0, rb)
-            return carry
-
-        lax.fori_loop(0, chunks, adjoint_step, 0)
+
+        if step:
+            start_outer, start_row, later = exchange(step % 2, -1)
+            sweep(adjoint_step, (step + 1) % 2, (start_outer, start_row), finish)
+            finish = later
+        else:
+            sweep(adjoint_step, 1, None, finish)
 
 
 def solution(mesh):
@@ -553,9 +598,12 @@
                 jax.ShapeDtypeStruct(checkpoint.shape, f32),
                 jax.ShapeDtypeStruct(resistance.shape, f32),
             ),
-            in_specs=[vmem, pl.BlockSpec(memory_space=pl.ANY), vmem, vmem],
+            in_specs=[pl.BlockSpec(memory_space=pltpu.HBM)] * 4,
             out_specs=(vmem, vmem),
             scratch_shapes=[
+                pltpu.VMEM(checkpoint.shape, f32),
+                pltpu.VMEM(resistance.shape, f32),
+                pltpu.VMEM(solid_mask.shape, jnp.int32),
                 pltpu.VMEM((3, 27) + padded, f32),
                 pltpu.VMEM((3, 27, ext_x, ext_y, lanes), f32),
                 pltpu.VMEM((27, ext_x, ext_y, lanes), f32),
@@ -577,10 +625,10 @@
                 pltpu.SemaphoreType.DMA((10,)),
                 pltpu.SemaphoreType.DMA((count,)),
                 pltpu.SemaphoreType.DMA((count,)),
-                pltpu.SemaphoreType.DMA,
+                pltpu.SemaphoreType.DMA((4,)),
             ],
             compiler_params=pltpu.CompilerParams(
-                collective_id=0, has_side_effects=True, vmem_limit_bytes=48 * 1024 * 1024
+                collective_id=0, has_side_effects=True, vmem_limit_bytes=60 * 1024 * 1024
             ),
         )(checkpoint, later_adjoint, resistance, solid_mask)
 

time: 56.5 us -> 50.5 us (0.89)
  Pallas kernels: 50.1 us -> 46.9 us
  local copies, waits for them, and re-layouts: 5.37 us -> 2.8 us
    pallas_call x1, Pallas kernels: 50.1 us -> 46.9 us  [shards(): pl.pallas_call(functools.partial(kernel, nx, ny), out_shape=(jax.ShapeDty...]
    unnamed x10 -> x4, local copies, waits for them, and re-layouts: 5.37 us -> 2.8 us
where the time goes in v1:
time: 50.5 us; the launch traced here: 50.4 us
  Pallas kernels  46.9 us (93%)
  local copies, waits for them, and re-layouts  2.8 us (6%)
  between operations  0.65 us (1%)
    pallas_call x1, Pallas kernels, shards(): pl.pallas_call(functools.partial(kernel, nx, ny), out_shape=(jax.ShapeDty...  46.9 us
    unnamed x4, local copies, waits for them, and re-layouts  2.8 us

profile of v1, /device:TPU:0, one launch (start us, length us, event | category | flops | bytes accessed | tf_op | source)
XLA Modules:
  0.0 50.4 jit_solution(14339629624227170980)
XLA Ops:
  0.6 46.9 %shard_map.59 = (f32[27,4,16,128]{3,2,1,0:T(8,128)}, f32[4,16,128]{2,1,0:T(8,128)}) custom-call(f32[27,4,16,128]{3,2,1,0:T(8,128)} %cp_hbm.1, f32[27,4,16,128]{3,2,1,0:T(8,128)} %la_ref.1, f32[4,16,128]{2,1,0:T(8,128)} %res_hbm.1, s32[4,16,128]{2,1,0:T(8,128)} %mask_hbm.1), custom_call_target="tpu_custom_call" | custom-call | tf_op jit(solution)/shard_map/pallas_call | solution.py:595
  47.5 0.0 copy-start
  47.6 2.2 %copy.8 = f32[27,4,16,128]{3,2,1,0:T(8,128)} copy(f32[27,4,16,128]{3,2,1,0:T(8,128)} %get-tuple-element.4) | data formatting | bytes 1769472
  49.7 0.0 copy-done
  49.7 0.6 %copy.9 = f32[4,16,128]{2,1,0:T(8,128)} copy(f32[4,16,128]{2,1,0:T(8,128)S(1)} %copy-done) | data formatting | bytes 65536
Async XLA Ops:
  47.5 2.2 %copy-start = (f32[4,16,128]{2,1,0:T(8,128)S(1)}, f32[4,16,128]{2,1,0:T(8,128)}, u32[]{:S(2)}) copy-start(f32[4,16,128]{2,1,0:T(8,128)} %get-tuple-element.5) | copy-start | bytes 98308
